TPU v7x, 256 devices: a whole 4x4x8 slice. The times are simulated.
256 devices in a mesh: ctx: 32 (over z, y), dp: 8 (over x, core).
Axes of the slice: x: 4, y: 4, z: 8, core: 2. Of those that a mesh axis runs over, the one named last changes fastest.
Arguments:
- queries: bfloat16 [24576, 8192], P('ctx', 'dp'), may hold values from -96 to 96
- keys: bfloat16 [24576, 1024], P(('ctx', 'dp')), may hold values from -36 to 36
- values: bfloat16 [24576, 1024], P(('ctx', 'dp')), may hold values from -6 to 6
- grad_out: bfloat16 [24576, 8192], P('ctx', 'dp'), may hold values from -6 to 6
- doc_lengths: int32 [64], replicated, may hold values from 1 to 768, 24576 in all
Outputs:
- attn_out: bfloat16 [24576, 8192], P('ctx', 'dp')
- grad_q: bfloat16 [24576, 8192], P('ctx', 'dp')
- grad_k: bfloat16 [24576, 1024], P(('ctx', 'dp'))
- grad_v: bfloat16 [24576, 1024], P(('ctx', 'dp'))
Inputs may be any that keep to these rules, and one draw needn't show every extreme that they name: `doc_lengths`: the lengths sum to 24576.
All inputs are finite; a program needn't handle non-finite values.
Results may differ from a plain program's by a relative error of at most 0.02.
Values may be sent and summed in bfloat16 or wider, within the bound.
No kernel may reach another device: no remote copies, remote signals or barrier semaphores. Data moves between devices by JAX's collectives and lax.ppermute only.
A program may use at most 64 MiB of HBM per device.

v0:
```python
import functools
import math

import jax
import jax.numpy as jnp
from jax import lax
from jax.experimental import pallas as pl
from jax.experimental.pallas import tpu as pltpu
from jax.sharding import PartitionSpec as P

HD = 128
TILE = 128
NEG = -1e30
F32 = jnp.float32
BF16 = jnp.bfloat16
SCALE = 1.0 / math.sqrt(HD)
LOG2_SCALE = SCALE * math.log2(math.e)


def dot_nt(a, b):
    return lax.dot_general(a, b, (((1,), (1,)), ((), ())), preferred_element_type=F32)


def dot_nn(a, b):
    return lax.dot_general(a, b, (((1,), (0,)), ((), ())), preferred_element_type=F32)


def by_rows(ref, heads=None):
    heads = range(ref.shape[1] // HD) if heads is None else heads
    return jnp.concatenate([ref[:, h * HD:(h + 1) * HD] for h in heads], axis=0)


def put_rows(ref, x, heads=None):
    heads = range(ref.shape[1] // HD) if heads is None else heads
    for j, h in enumerate(heads):
        ref[:, h * HD:(h + 1) * HD] = x[j * TILE:(j + 1) * TILE].astype(ref.dtype)


def head_groups(heads, count):
    size = heads // count
    return [(range(j * size, (j + 1) * size), slice(j * size * TILE, (j + 1) * size * TILE)) for j in range(count)]


def write_bias(bias_ref, start_ref, first, count, offset, causal):
    startc = jnp.transpose(jnp.broadcast_to(start_ref[0], (TILE, TILE)))
    lane = lax.broadcasted_iota(jnp.int32, (TILE, TILE), 1)
    row = lax.broadcasted_iota(jnp.int32, (TILE, TILE), 0)
    for j in range(count):
        keep = lane >= startc - ((first + j) * TILE + offset)
        if causal and j == count - 1:
            keep = keep & (lane <= row)
        bias_ref[:, j * TILE:(j + 1) * TILE] = jnp.where(keep, 0.0, NEG)


def biased_scores(q, k, bias, heads):
    t = dot_nt(q, k) * LOG2_SCALE
    rows, width = t.shape
    return (t.reshape(heads, TILE, width) + bias[None]).reshape(rows, width)


def key_tiles(first_ref, i, tiles):
    first = lax.div(first_ref[i], TILE)
    return jnp.minimum(tiles + i - first, i) + 1, jnp.maximum(tiles - first, 0)


def local_forward(first_ref, start_ref, q_ref, g_ref, kv_ref, p_ref, o_ref, max_ref, out_ref, gs_ref, v_s, bias_s):
    i = pl.program_id(0)
    tiles = pl.num_programs(0)
    rows = kv_ref.shape[0]
    heads = q_ref.shape[1] // HD
    here, before = key_tiles(first_ref, i, tiles)

    @pl.when(i == 0)
    def _():
        v_s[:, :HD] = kv_ref[:, HD:]
        v_s[:, HD:] = jnp.ones((rows, HD), BF16)

    for w in range(1, rows // TILE + 1):
        @pl.when(here == w)
        def _(w=w):
            first = i - (w - 1)
            write_bias(bias_s, start_ref, first, w, rows, True)
            keys = pl.ds(pl.multiple_of(first * TILE, TILE), w * TILE)
            for hs, at in head_groups(heads, 2 if w > 3 else 1):
                t = biased_scores(by_rows(q_ref, hs), kv_ref[keys, :HD], bias_s[:, :w * TILE], len(hs))
                m = jnp.max(t, axis=1, keepdims=True)
                p = jnp.exp2(t - m).astype(BF16)
                p_ref[i, at, :w * TILE] = p
                o_ref[i, at] = dot_nn(p, v_s[keys, :])
                max_ref[i, at] = jnp.broadcast_to(m, (m.shape[0], HD))

    @pl.when(before == 0)
    def _():
        finish_rows(o_ref, g_ref, out_ref, gs_ref, i)


def finish_rows(o_ref, g_ref, out_ref, gs_ref, i):
    inv = 1.0 / o_ref[i, :, HD:]
    put_rows(out_ref, o_ref[i, :, :HD] * inv)
    put_rows(gs_ref, by_rows(g_ref).astype(F32) * inv)


def prev_step(first_ref, start_ref, q_ref, g_ref, kv_ref, o_ref, max_ref, out_any, gs_any,
              out_ref, gs_ref, ds_ref, dkv_ref, v_s, bias_s, dk_s, dv_s):
    i = pl.program_id(0)
    rows = kv_ref.shape[0]
    tiles = rows // TILE
    heads = q_ref.shape[1] // HD
    before = key_tiles(first_ref, i, tiles)[1]

    @pl.when(i == 0)
    def _():
        v_s[:, :HD] = kv_ref[:, HD:]
        v_s[:, HD:] = jnp.ones((rows, HD), BF16)
        dk_s[...] = jnp.zeros_like(dk_s)
        dv_s[...] = jnp.zeros_like(dv_s)

    @pl.when((i == 0) & (before == 0))
    def _():
        finish_rows(o_ref, g_ref, out_ref, gs_ref, 0)

    for w in range(1, rows // TILE + 1):
        @pl.when(before == w)
        def _(w=w):
            first = rows // TILE - w
            write_bias(bias_s, start_ref, first, w, 0, False)
            keys = slice(first * TILE, rows)
            for hs, at in head_groups(heads, 1):
                q = by_rows(q_ref, hs)
                g = by_rows(g_ref, hs).astype(F32)
                t = biased_scores(q, kv_ref[keys, :HD], bias_s[:, :w * TILE], len(hs))
                m1 = max_ref[i, at]
                m = jnp.maximum(m1, jnp.max(t, axis=1, keepdims=True))
                a1 = jnp.exp2(m1 - m)
                p = jnp.exp2(t - jnp.concatenate([m] * w, axis=1))
                pb = p.astype(BF16)
                o2 = dot_nn(pb, v_s[keys, :])
                inv = 1.0 / (a1 * o_ref[i, at, HD:] + o2[:, HD:])
                out = ((a1 * o_ref[i, at, :HD] + o2[:, :HD]) * inv).astype(BF16)
                g = g * inv
                gs = g.astype(BF16)
                put_rows(out_ref, out, hs)
                put_rows(gs_ref, g * a1, hs)
                delta = jnp.sum(gs.astype(F32) * out.astype(F32), axis=1, keepdims=True)
                ds = (p * (dot_nt(gs, kv_ref[keys, HD:]) - delta)).astype(BF16)
                ds_ref[i, at, :w * TILE] = ds
                add_grads(dk_s, dv_s, first, w, dot_nn(jnp.transpose(q), ds), dot_nn(jnp.transpose(gs), pb))

    @pl.when(i == pl.num_programs(0) - 1)
    def _():
        write_grads(dkv_ref, dk_s, dv_s, key_tiles(first_ref, 0, tiles)[1])


def add_grads(dk_s, dv_s, first, count, dk, dv):
    for j in range(count):
        dk_s[first + j] += dk[:, j * TILE:(j + 1) * TILE]
        dv_s[first + j] += dv[:, j * TILE:(j + 1) * TILE]


def write_grads(ref, dk_s, dv_s, count):
    tiles = dk_s.shape[0]
    for j in range(tiles):
        at = slice(j * TILE, (j + 1) * TILE)

        @pl.when(j >= tiles - count)
        def _(j=j, at=at):
            ref[at, :HD] = (jnp.transpose(dk_s[j]) * SCALE).astype(ref.dtype)
            ref[at, HD:] = jnp.transpose(dv_s[j]).astype(ref.dtype)

        @pl.when(j < tiles - count)
        def _(at=at):
            ref[at, :] = jnp.zeros((TILE, 2 * HD), ref.dtype)


def local_backward(first_ref, q_ref, gs_ref, out_ref, p_ref, dsp_ref, kvp_ref, kv_ref, dq_ref, dkv_ref, dk_s, dv_s):
    i = pl.program_id(0)
    tiles = pl.num_programs(0)
    rows = kv_ref.shape[0]
    here, before = key_tiles(first_ref, i, tiles)

    @pl.when(i == 0)
    def _():
        dk_s[...] = jnp.zeros_like(dk_s)
        dv_s[...] = jnp.zeros_like(dv_s)

    for w in range(1, rows // TILE + 1):
        @pl.when(here == w)
        def _(w=w):
            first = i - (w - 1)
            keys = pl.ds(pl.multiple_of(first * TILE, TILE), w * TILE)
            for hs, at in head_groups(q_ref.shape[1] // HD, 1):
                q = by_rows(q_ref, hs)
                gs = by_rows(gs_ref, hs)
                pb = p_ref[i, at, :w * TILE]
                delta = jnp.sum(gs.astype(F32) * by_rows(out_ref, hs).astype(F32), axis=1, keepdims=True)
                ds = (pb.astype(F32) * (dot_nt(gs, kv_ref[keys, HD:]) - delta)).astype(BF16)
                put_rows(dq_ref, dot_nn(ds, kv_ref[keys, :HD]) * SCALE, hs)
                add_grads(dk_s, dv_s, first, w, dot_nn(jnp.transpose(q), ds), dot_nn(jnp.transpose(gs), pb))

    for w in range(1, rows // TILE + 1):
        @pl.when(before == w)
        def _(w=w):
            dq = dot_nn(dsp_ref[i, :, :w * TILE], kvp_ref[rows - w * TILE:, :HD]) * SCALE
            put_rows(dq_ref, by_rows(dq_ref).astype(F32) + dq)

    @pl.when(i == tiles - 1)
    def _():
        write_grads(dkv_ref, dk_s, dv_s, tiles)


def call(body, name, rows, steps, ins, outs, scratch, flops, limit, aliases={}):
    big = rows * 4 * HD

    def in_hbm(x):
        if isinstance(x, jax.ShapeDtypeStruct) and math.prod(x.shape) >= big:
            return pltpu.HBM(x.shape, x.dtype)
        return x

    run = pl.pallas_call(
        body,
        grid_spec=pltpu.PrefetchScalarGridSpec(
            num_scalar_prefetch=1, grid=(steps,), in_specs=ins, out_specs=[s for s, _ in outs], scratch_shapes=scratch
        ),
        out_shape=[in_hbm(s) for _, s in outs],
        input_output_aliases=aliases,
        compiler_params=pltpu.CompilerParams(dimension_semantics=("arbitrary",), vmem_limit_bytes=limit << 20),
        cost_estimate=pl.CostEstimate(flops=flops, transcendentals=0, bytes_accessed=8 << 20),
        name=name,
    )
    return lambda n, *args: run(n, *[pltpu.with_memory_space_constraint(x, pltpu.HBM) if x.ndim == 2 and x.size >= big else x for x in args])


def attention_calls(first, starts, q, g):
    rows, width = q.shape
    tiles = rows // TILE
    sds = jax.ShapeDtypeStruct
    own_tile = lambda i, n: i
    met_tile = lambda i, n: n[tiles + i]
    whole = pl.BlockSpec((rows, 2 * HD), lambda i, n: (0, 0))

    def flat(at, w=width):
        return pl.BlockSpec((TILE, w), lambda i, n: (at(i, n), 0))

    def slab(at, *dims):
        return pl.BlockSpec((1,) + dims, lambda i, n: (at(i, n), 0, 0))

    held = pl.BlockSpec(memory_space=pltpu.VMEM)
    there = pl.BlockSpec(memory_space=pl.ANY)
    grads = [pltpu.VMEM((tiles, HD, TILE), F32)] * 2
    shared = [pltpu.VMEM((rows, 2 * HD), BF16), pltpu.VMEM((TILE, rows), F32)]
    rows_bf16 = sds((rows, width), BF16)

    def forward_local(own):
        return call(
            local_forward, "local_forward", rows, tiles,
            [slab(own_tile, 1, TILE), flat(own_tile), flat(own_tile), whole],
            [
                (held, pltpu.VMEM((tiles, width, rows), BF16)),
                (held, pltpu.VMEM((tiles, width, 2 * HD), F32)),
                (held, pltpu.VMEM((tiles, width, HD), F32)),
                (flat(own_tile), rows_bf16),
                (flat(own_tile), rows_bf16),
            ],
            shared, 3 << 30, 24,
        )(first, starts, q, g, own)

    def finish_prev(prev, o, maxes, out, gs):
        return call(
            prev_step, "previous_block", rows, tiles,
            [
                slab(met_tile, 1, TILE), flat(met_tile), flat(met_tile), whole,
                held, held, there, there,
            ],
            [
                (flat(met_tile), rows_bf16), (flat(met_tile), rows_bf16),
                (held, pltpu.VMEM((tiles, width, rows), BF16)), (whole, sds((rows, 2 * HD), BF16)),
            ],
            shared + grads, 4 << 30, 24, {7: 0, 8: 1},
        )(first, starts, q, g, prev, o, maxes, out, gs)

    def backward_local(gs, out, p, dsp, prev, own):
        return call(
            local_backward, "local_backward", rows, tiles,
            [flat(own_tile), flat(own_tile), flat(own_tile), held, held, whole, whole],
            [(flat(own_tile), rows_bf16), (whole, sds((rows, 2 * HD), F32))],
            grads, 5 << 30, 24,
        )(first, q, gs, out, p, dsp, prev, own)

    return forward_local, finish_prev, backward_local


def pack_kernel(k_ref, v_ref, out_ref):
    for h in range(out_ref.shape[0]):
        out_ref[h, :, :HD] = k_ref[:, h * HD:(h + 1) * HD]
        out_ref[h, :, HD:] = v_ref[:, h * HD:(h + 1) * HD]


def unpack_kernel(x_ref, k_ref, v_ref):
    for h in range(x_ref.shape[0]):
        k_ref[:, h * HD:(h + 1) * HD] = x_ref[h, :, :HD]
        v_ref[:, h * HD:(h + 1) * HD] = x_ref[h, :, HD:]


def pack(keys, values):
    tokens, width = keys.shape
    heads = width // HD
    half = pl.BlockSpec((tokens, width // 2), lambda i: (0, i))
    return pl.pallas_call(
        pack_kernel,
        grid=(2,),
        in_specs=[half, half],
        out_specs=pl.BlockSpec((heads // 2, tokens, 2 * HD), lambda i: (i, 0, 0)),
        out_shape=jax.ShapeDtypeStruct((heads, tokens, 2 * HD), BF16),
        name="pack_heads",
    )(keys, values)


def unpack(x):
    heads, tokens, _ = x.shape
    return pl.pallas_call(
        unpack_kernel,
        in_specs=[pl.BlockSpec(memory_space=pltpu.VMEM)],
        out_shape=[jax.ShapeDtypeStruct((tokens, heads * HD), BF16)] * 2,
        name="unpack_heads",
    )(pltpu.with_memory_space_constraint(x, pltpu.VMEM))


def passed_along(x, axis, by, ring):
    count = lax.axis_size(axis)
    pairs = [(i, (i + by) % count) for i in range(count) if ring or 0 <= i + by < count]
    return lax.ppermute(x, axis, pairs)


def per_device(queries, keys, values, grad_out, doc_lengths):
    rows = queries.shape[0]
    shared = pack(keys, values)
    own = lax.all_to_all(shared, "dp", split_axis=0, concat_axis=0, tiled=True).reshape(rows, 2 * HD)
    first_pos = lax.axis_index("ctx") * rows
    ends = jnp.cumsum(doc_lengths)
    positions = first_pos + jnp.arange(rows, dtype=jnp.int32)
    starts = jnp.max(jnp.where(ends[None, :] <= positions[:, None], ends[None, :], 0), axis=1)
    starts = (starts - first_pos + rows).astype(jnp.int32)
    tiles = rows // TILE
    first = starts[::TILE]
    crossing = jnp.sum(first < rows, dtype=jnp.int32)
    met = jnp.minimum(jnp.arange(tiles, dtype=jnp.int32), jnp.maximum(crossing - 1, 0))
    first = jnp.concatenate([first, met])
    own, first = lax.optimization_barrier((own, first))
    prev = passed_along(own, "ctx", 1, True)
    forward_local, finish_prev, backward_local = attention_calls(
        first, starts.reshape(tiles, 1, TILE), queries, grad_out
    )
    probs, sums, maxes, out, scaled = forward_local(own)
    attn_out, scaled, grad_scores, back = finish_prev(prev, sums, maxes, out, scaled)
    grad_q, mine = backward_local(scaled, attn_out, probs, grad_scores, prev, own)
    total = (mine + passed_along(back, "ctx", -1, False).astype(F32)).astype(BF16)
    total = total.reshape(shared.shape)
    grads = lax.all_to_all(total, "dp", split_axis=0, concat_axis=0, tiled=True)
    grad_k, grad_v = unpack(grads)
    return attn_out, grad_q, grad_k, grad_v


def solution(mesh):
    placed = (P("ctx", "dp"), P(("ctx", "dp"), None), P(("ctx", "dp"), None), P("ctx", "dp"), P())
    return jax.shard_map(
        per_device,
        mesh=mesh,
        in_specs=placed,
        out_specs=(P("ctx", "dp"), P("ctx", "dp"), P(("ctx", "dp"), None), P(("ctx", "dp"), None)),
        check_vma=False,
    )
```

profile of v0, /device:TPU:120, one launch (start us, length us, event | category | flops | bytes accessed | tf_op | source)
XLA Modules:
  0.0 63.7 jit_solution(14949784448768094570)
XLA Ops:
  0.6 0.0 copy-start
  0.6 1.8 %pack_heads.1 = bf16[8,96,256]{2,1,0:T(8,128)(2,1)} custom-call(bf16[96,1024]{1,0:T(8,128)(2,1)} %k_ref.1, bf16[96,1024]{1,0:T(8,128)(2,1)} %v_ref.1), custom_call_target="tpu_custom_call" | custom-call | tf_op jit(solution)/shard_map/pack_heads/pallas_call | solution.py:308
  2.4 4.3 %all-to-all-start = ((bf16[8,96,256]{2,1,0:T(8,128)(2,1)}), bf16[8,96,256]{2,1,0:T(8,128)(2,1)S(1)}, u32[]{:S(2)}, u32[]{:S(2)}) async-start(bf16[8,96,256]{2,1,0:T(8,128)(2,1)} %pack_heads.1), calls=%async_computation | async-start | bytes 786432 | tf_op jit(solution)/shard_map/all_to_all | solution.py:337
  6.7 0.0 copy-done
  6.7 0.1 copy.13
  6.8 0.1 reduce-window.8
  6.9 0.1 reduce
  7.0 0.1 select_reduce_fusion
  7.2 0.1 slice.3
  7.2 0.6 fusion
  8.5 0.1 pad_add_fusion.first_ref
  8.6 7.0 %all-to-all-done = bf16[8,96,256]{2,1,0:T(8,128)(2,1)S(1)} async-done(((bf16[8,96,256]{2,1,0:T(8,128)(2,1)}), bf16[8,96,256]{2,1,0:T(8,128)(2,1)S(1)}, u32[]{:S(2)}, u32[]{:S(2)}) %all-to-all-start) | async-done | bytes 393248 | tf_op jit(solution)/shard_map/all_to_all | solution.py:337
  15.7 2.8 %collective-permute-start = (bf16[768,256]{1,0:T(8,128)(2,1)S(1)}, bf16[768,256]{1,0:T(8,128)(2,1)S(1)}, u32[]{:S(2)}, u32[]{:S(2)}) collective-permute-start(bf16[768,256]{1,0:T(8,128)(2,1)S(1)} %bitcast.3), channel_id=1, source_target_pairs={{0,8},{8,16},{16,24},{24,32},{32,40},{40,48},{48,56},{56,64},{64,7... | collective-permute-start | bytes 1179656 | tf_op jit(solution)/shard_map/ppermute | solution.py:331
  18.4 8.8 %local_forward.1 = (bf16[6,1024,768]{2,1,0:T(8,128)(2,1)S(1)}, f32[6,1024,256]{2,1,0:T(8,128)S(1)}, f32[6,1024,128]{2,1,0:T(8,128)S(1)}, bf16[768,1024]{1,0:T(8,128)(2,1)}, bf16[768,1024]{1,0:T(8,128)(2,1)}) custom-call(s32[12]{0:T(128)S(1)} %pad_add_fusion.first_ref, s32[6,1,128]{2,1,0:T(1,128)S(1)} %add.34.start_ref, bf16[768,1024]{1,0:T(8,128)(2,1)} %q_ref.5, ...), custom_call_target="tpu_custom_call" | custom-call | flops 3221225472 | bytes 8388608 | tf_op jit(solution)/shard_map/local_forward/pallas_call | solution.py:230
  27.2 0.0 collective-permute-done.kv_ref.kvp_ref
  27.2 8.6 %previous_block.1 = (bf16[768,1024]{1,0:T(8,128)(2,1)}, bf16[768,1024]{1,0:T(8,128)(2,1)}, bf16[6,1024,768]{2,1,0:T(8,128)(2,1)S(1)}, bf16[768,256]{1,0:T(8,128)(2,1)S(1)}) custom-call(s32[12]{0:T(128)S(1)} %pad_add_fusion.first_ref, s32[6,1,128]{2,1,0:T(1,128)S(1)} %add.34.start_ref, ...), custom_call_target="tpu_custom_call", output_to_operand_aliasing={{0}: (7, {}), {1}: (8, {})} | custom-call | flops 4294967296 | bytes 8388608 | tf_op jit(solution)/shard_map/previous_block/pallas_call | solution.py:230
  35.9 1.9 %collective-permute-start.1 = (bf16[768,256]{1,0:T(8,128)(2,1)S(1)}, bf16[768,256]{1,0:T(8,128)(2,1)S(1)}, u32[]{:S(2)}, u32[]{:S(2)}) collective-permute-start(bf16[768,256]{1,0:T(8,128)(2,1)S(1)} %get-tuple-element.31), channel_id=1, source_target_pairs={{8,0},{16,8},{24,16},{32,24},{40,32},{48,40},{56,48},{64,56},{72,6... | collective-permute-start | bytes 1179656 | tf_op jit(solution)/shard_map/ppermute | solution.py:331
  37.8 9.8 %local_backward.1 = (bf16[768,1024]{1,0:T(8,128)(2,1)}, f32[768,256]{1,0:T(8,128)S(1)}) custom-call(s32[12]{0:T(128)S(1)} %pad_add_fusion.first_ref, bf16[768,1024]{1,0:T(8,128)(2,1)} %q_ref.5, bf16[768,1024]{1,0:T(8,128)(2,1)} %get-tuple-element.26.gs_ref, bf16[768,1024]{1,0:T(8,128)(2,1)} %get-tuple-element.15.out_ref, ...), custom_call_target="tpu_custom_call" | custom-call | flops 5368709120 | bytes 8388608 | tf_op jit(solution)/shard_map/local_backward/pallas_call | solution.py:230
  47.6 3.9 %collective-permute-done.1 = bf16[768,256]{1,0:T(8,128)(2,1)S(1)} collective-permute-done((bf16[768,256]{1,0:T(8,128)(2,1)S(1)}, bf16[768,256]{1,0:T(8,128)(2,1)S(1)}, u32[]{:S(2)}, u32[]{:S(2)}) %collective-permute-start.1) | collective-permute-done | bytes 393248 | tf_op jit(solution)/shard_map/ppermute | solution.py:331
  51.5 0.1 add_convert_fusion
  51.5 11.3 %all_to_all.10.x_ref = bf16[8,96,256]{2,1,0:T(8,128)(2,1)S(1)} all-to-all(bf16[8,96,256]{2,1,0:T(8,128)(2,1)S(1)} %bitcast.6), channel_id=1, replica_groups=mesh['ctx'=32,'dp'=8] {'dp'}, dimensions={0} | all-to-all | bytes 786432 | tf_op jit(solution)/shard_map/all_to_all | solution.py:358
  62.9 0.9 %unpack_heads.1 = (bf16[96,1024]{1,0:T(8,128)(2,1)}, bf16[96,1024]{1,0:T(8,128)(2,1)}) custom-call(bf16[8,96,256]{2,1,0:T(8,128)(2,1)S(1)} %all_to_all.10.x_ref), custom_call_target="tpu_custom_call" | custom-call | tf_op jit(solution)/shard_map/unpack_heads/pallas_call | solution.py:320
  (4 shorter events, 0.0 us)
Async XLA Ops:
  0.6 6.1 %copy-start = (s32[64]{0:T(128)S(1)}, s32[64]{0:T(128)}, u32[]{:S(2)}) copy-start(s32[64]{0:T(128)} %param.9) | copy-start | bytes 772
  2.4 13.2 %all-to-all-start = ((bf16[8,96,256]{2,1,0:T(8,128)(2,1)}), bf16[8,96,256]{2,1,0:T(8,128)(2,1)S(1)}, u32[]{:S(2)}, u32[]{:S(2)}) async-start(bf16[8,96,256]{2,1,0:T(8,128)(2,1)} %pack_heads.1), calls=%async_computation | async-start | bytes 786432 | tf_op jit(solution)/shard_map/all_to_all | solution.py:337
  15.7 11.6 %collective-permute-start = (bf16[768,256]{1,0:T(8,128)(2,1)S(1)}, bf16[768,256]{1,0:T(8,128)(2,1)S(1)}, u32[]{:S(2)}, u32[]{:S(2)}) collective-permute-start(bf16[768,256]{1,0:T(8,128)(2,1)S(1)} %bitcast.3), channel_id=1, source_target_pairs={{0,8},{8,16},{16,24},{24,32},{32,40},{40,48},{48,56},{56,64},{64,7... | collective-permute-start | bytes 1179656 | tf_op jit(solution)/shard_map/ppermute | solution.py:331
  35.9 15.6 %collective-permute-start.1 = (bf16[768,256]{1,0:T(8,128)(2,1)S(1)}, bf16[768,256]{1,0:T(8,128)(2,1)S(1)}, u32[]{:S(2)}, u32[]{:S(2)}) collective-permute-start(bf16[768,256]{1,0:T(8,128)(2,1)S(1)} %get-tuple-element.31), channel_id=1, source_target_pairs={{8,0},{16,8},{24,16},{32,24},{40,32},{48,40},{56,48},{64,56},{72,6... | collective-permute-start | bytes 1179656 | tf_op jit(solution)/shard_map/ppermute | solution.py:331
where the time goes:
time: 63.8 us; the launch traced here: 63.7 us
  Pallas kernels  29.8 us (47%)
  blocking collectives  11.3 us (18%)
  waiting for transfers between devices  10.9 us (17%)
  starting transfers between devices  9 us (14%)
  between operations  1.35 us (2%)
  other arithmetic  1.13 us (2%)
    pallas_call x3, Pallas kernels, call(): run(n, *[pltpu.with_memory_space_constraint(x, pltpu.HBM) if x.ndim == 2...  27.2 us
    all_to_all x1, blocking collectives, per_device(): grads = lax.all_to_all(total, 'dp', split_axis=0, concat_axis=0, tiled=True)  11.3 us
    all_to_all x1, waiting for transfers between devices, per_device(): lax.all_to_all(shared, 'dp', split_axis=0, concat_axis=0, tiled=True)  7.02 us
    ppermute x2, starting transfers between devices, passed_along(): return lax.ppermute(x, axis, pairs)  4.7 us
    all_to_all x1, starting transfers between devices, per_device(): lax.all_to_all(shared, 'dp', split_axis=0, concat_axis=0, tiled=True)  4.3 us
    ppermute x2, waiting for transfers between devices, passed_along(): return lax.ppermute(x, axis, pairs)  3.87 us
    pallas_call x1, Pallas kernels, pack(): pl.pallas_call(pack_kernel, grid=(2,), in_specs=[half, half], out_specs=p...  1.76 us
  transfers between devices with their start and end apart: 3, of which 2 were waited for; matrix products, arithmetic and copies ran while one was open for 2% of the time, Pallas kernels for 29%

commit v1 on v0

--- a/solution.py
+++ b/solution.py
@@ -211,7 +211,7 @@
 def call(body, name, rows, steps, ins, outs, scratch, flops, limit, aliases={}):
     big = rows * 4 * HD
 
-    def in_hbm(x):
+    def placed(x):
         if isinstance(x, jax.ShapeDtypeStruct) and math.prod(x.shape) >= big:
             return pltpu.HBM(x.shape, x.dtype)
         return x
@@ -221,18 +221,24 @@
         grid_spec=pltpu.PrefetchScalarGridSpec(
             num_scalar_prefetch=1, grid=(steps,), in_specs=ins, out_specs=[s for s, _ in outs], scratch_shapes=scratch
         ),
-        out_shape=[in_hbm(s) for _, s in outs],
+        out_shape=[placed(s) for _, s in outs],
         input_output_aliases=aliases,
         compiler_params=pltpu.CompilerParams(dimension_semantics=("arbitrary",), vmem_limit_bytes=limit << 20),
         cost_estimate=pl.CostEstimate(flops=flops, transcendentals=0, bytes_accessed=8 << 20),
         name=name,
     )
-    return lambda n, *args: run(n, *[pltpu.with_memory_space_constraint(x, pltpu.HBM) if x.ndim == 2 and x.size >= big else x for x in args])
+    return run
+
+
+def in_hbm(x):
+    return pltpu.with_memory_space_constraint(x, pltpu.HBM)
 
 
 def attention_calls(first, starts, q, g):
     rows, width = q.shape
     tiles = rows // TILE
+    q = pltpu.with_memory_space_constraint(q, pltpu.VMEM)
+    g_near = pltpu.with_memory_space_constraint(g, pltpu.VMEM)
     sds = jax.ShapeDtypeStruct
     own_tile = lambda i, n: i
     met_tile = lambda i, n: n[tiles + i]
@@ -249,6 +255,7 @@
     grads = [pltpu.VMEM((tiles, HD, TILE), F32)] * 2
     shared = [pltpu.VMEM((rows, 2 * HD), BF16), pltpu.VMEM((TILE, rows), F32)]
     rows_bf16 = sds((rows, width), BF16)
+    near_bf16 = pltpu.VMEM((rows, width), BF16)
 
     def forward_local(own):
         return call(
@@ -259,12 +266,13 @@
                 (held, pltpu.VMEM((tiles, width, 2 * HD), F32)),
                 (held, pltpu.VMEM((tiles, width, HD), F32)),
                 (flat(own_tile), rows_bf16),
-                (flat(own_tile), rows_bf16),
+                (flat(own_tile), near_bf16),
             ],
-            shared, 3 << 30, 24,
-        )(first, starts, q, g, own)
+            shared, 3 << 30, 16,
+        )(first, starts, q, in_hbm(g), own)
 
     def finish_prev(prev, o, maxes, out, gs):
+        out = in_hbm(out)
         return call(
             prev_step, "previous_block", rows, tiles,
             [
@@ -272,18 +280,19 @@
                 held, held, there, there,
             ],
             [
-                (flat(met_tile), rows_bf16), (flat(met_tile), rows_bf16),
+                (flat(met_tile), rows_bf16), (flat(met_tile), near_bf16),
                 (held, pltpu.VMEM((tiles, width, rows), BF16)), (whole, sds((rows, 2 * HD), BF16)),
             ],
-            shared + grads, 4 << 30, 24, {7: 0, 8: 1},
-        )(first, starts, q, g, prev, o, maxes, out, gs)
+            shared + grads, 4 << 30, 16, {7: 0, 8: 1},
+        )(first, starts, q, g_near, prev, o, maxes, out, gs)
 
     def backward_local(gs, out, p, dsp, prev, own):
+        out = in_hbm(out)
         return call(
             local_backward, "local_backward", rows, tiles,
             [flat(own_tile), flat(own_tile), flat(own_tile), held, held, whole, whole],
             [(flat(own_tile), rows_bf16), (whole, sds((rows, 2 * HD), F32))],
-            grads, 5 << 30, 24,
+            grads, 5 << 30, 16,
         )(first, q, gs, out, p, dsp, prev, own)
 
     return forward_local, finish_prev, backward_local

time: 63.8 us -> 62.9 us (0.986)
  Pallas kernels: 29.8 us -> 28.8 us
    pallas_call x3, Pallas kernels: 27.2 us -> 26 us  [the longest x1 9.48 us: backward_local(): call(local_backward, 'local_backward', rows, tiles, [flat(own_tile), flat...]
  transfers between devices with their start and end apart: 3 -> 3, of which waited for: 2 -> 2; matrix products, arithmetic and copies ran while one was open for 2% -> 2% of each run, Pallas kernels for 29% -> 28%
where the time goes in v1:
time: 62.9 us; the launch traced here: 63 us
  Pallas kernels  28.8 us (46%)
  blocking collectives  11.3 us (18%)
  waiting for transfers between devices  11.2 us (18%)
  starting transfers between devices  9 us (14%)
  between operations  1.36 us (2%)
  other arithmetic  1.13 us (2%)
    all_to_all x1, blocking collectives, per_device(): grads = lax.all_to_all(total, 'dp', split_axis=0, concat_axis=0, tiled=True)  11.3 us
    pallas_call x1, Pallas kernels, backward_local(): call(local_backward, 'local_backward', rows, tiles, [flat(own_tile), flat...  9.48 us
    pallas_call x1, Pallas kernels, forward_local(): call(local_forward, 'local_forward', rows, tiles, [slab(own_tile, 1, TILE...  8.43 us
    pallas_call x1, Pallas kernels, finish_prev(): call(prev_step, 'previous_block', rows, tiles, [slab(met_tile, 1, TILE),...  8.12 us
    all_to_all x1, waiting for transfers between devices, per_device(): lax.all_to_all(shared, 'dp', split_axis=0, concat_axis=0, tiled=True)  7.02 us
    ppermute x2, starting transfers between devices, passed_along(): return lax.ppermute(x, axis, pairs)  4.7 us
    all_to_all x1, starting transfers between devices, per_device(): lax.all_to_all(shared, 'dp', split_axis=0, concat_axis=0, tiled=True)  4.3 us
    ppermute x2, waiting for transfers between devices, passed_along(): return lax.ppermute(x, axis, pairs)  4.19 us
  transfers between devices with their start and end apart: 3, of which 2 were waited for; matrix products, arithmetic and copies ran while one was open for 2% of the time, Pallas kernels for 28%

profile of v1, /device:TPU:120, one launch (start us, length us, event | category | flops | bytes accessed | tf_op | source)
XLA Modules:
  0.0 63.0 jit_solution(506965424216732158)
XLA Ops:
  0.6 0.0 copy-start.2
  0.6 0.0 copy-start
  0.7 1.9 %pack_heads.1 = bf16[8,96,256]{2,1,0:T(8,128)(2,1)} custom-call(bf16[96,1024]{1,0:T(8,128)(2,1)} %k_ref.1, bf16[96,1024]{1,0:T(8,128)(2,1)} %v_ref.1), custom_call_target="tpu_custom_call" | custom-call | tf_op jit(solution)/shard_map/pack_heads/pallas_call | solution.py:317
  2.5 4.3 %all-to-all-start = ((bf16[8,96,256]{2,1,0:T(8,128)(2,1)}), bf16[8,96,256]{2,1,0:T(8,128)(2,1)S(1)}, u32[]{:S(2)}, u32[]{:S(2)}) async-start(bf16[8,96,256]{2,1,0:T(8,128)(2,1)} %pack_heads.1), calls=%async_computation | async-start | bytes 786432 | tf_op jit(solution)/shard_map/all_to_all | solution.py:346
  6.8 0.0 copy-done.2
  6.8 0.1 copy.13
  6.9 0.1 reduce-window.8
  7.0 0.1 reduce
  7.1 0.1 select_reduce_fusion
  7.3 0.1 slice.3
  7.4 0.6 %fusion = s32[]{:T(128)} fusion(s32[6]{0:T(128)S(1)} %slice.3), kind=kLoop, calls=%fused_computation.5 | loop fusion | flops 17 | bytes 28 | tf_op jit(solution)/shard_map/reduce_sum | solution.py:354
  8.7 0.1 pad_add_fusion.first_ref
  8.7 7.0 %all-to-all-done = bf16[8,96,256]{2,1,0:T(8,128)(2,1)S(1)} async-done(((bf16[8,96,256]{2,1,0:T(8,128)(2,1)}), bf16[8,96,256]{2,1,0:T(8,128)(2,1)S(1)}, u32[]{:S(2)}, u32[]{:S(2)}) %all-to-all-start) | async-done | bytes 393248 | tf_op jit(solution)/shard_map/all_to_all | solution.py:346
  15.8 2.8 %collective-permute-start = (bf16[768,256]{1,0:T(8,128)(2,1)S(1)}, bf16[768,256]{1,0:T(8,128)(2,1)S(1)}, u32[]{:S(2)}, u32[]{:S(2)}) collective-permute-start(bf16[768,256]{1,0:T(8,128)(2,1)S(1)} %bitcast.3), channel_id=1, source_target_pairs={{0,8},{8,16},{16,24},{24,32},{32,40},{40,48},{48,56},{56,64},{64,7... | collective-permute-start | bytes 1179656 | tf_op jit(solution)/shard_map/ppermute | solution.py:340
  18.6 0.0 copy-done
  18.6 8.4 %local_forward.1 = (bf16[6,1024,768]{2,1,0:T(8,128)(2,1)S(1)}, f32[6,1024,256]{2,1,0:T(8,128)S(1)}, f32[6,1024,128]{2,1,0:T(8,128)S(1)}, bf16[768,1024]{1,0:T(8,128)(2,1)}, bf16[768,1024]{1,0:T(8,128)(2,1)S(1)}) custom-call(s32[12]{0:T(128)S(1)} %pad_add_fusion.first_ref, s32[6,1,128]{2,1,0:T(1,128)S(1)} %add.34.start_ref, bf16[768,1024]{1,0:T(8,128)(2,1)S(1)} %copy-done, ...), custom_call_target="tpu_custom_call" | custom-call | flops 3221225472 | bytes 8388608 | tf_op jit(solution)/shard_map/local_forward/pallas_call | solution.py:261
  27.0 0.0 collective-permute-done.kv_ref.kvp_ref
  27.0 8.1 %previous_block.1 = (bf16[768,1024]{1,0:T(8,128)(2,1)}, bf16[768,1024]{1,0:T(8,128)(2,1)S(1)}, bf16[6,1024,768]{2,1,0:T(8,128)(2,1)S(1)}, bf16[768,256]{1,0:T(8,128)(2,1)S(1)}) custom-call(s32[12]{0:T(128)S(1)} %pad_add_fusion.first_ref, s32[6,1,128]{2,1,0:T(1,128)S(1)} %add.34.start_ref, ...), custom_call_target="tpu_custom_call", output_to_operand_aliasing={{0}: (7, {}), {1}: (8, {})} | custom-call | flops 4294967296 | bytes 8388608 | tf_op jit(solution)/shard_map/previous_block/pallas_call | solution.py:276
  35.1 1.9 %collective-permute-start.1 = (bf16[768,256]{1,0:T(8,128)(2,1)S(1)}, bf16[768,256]{1,0:T(8,128)(2,1)S(1)}, u32[]{:S(2)}, u32[]{:S(2)}) collective-permute-start(bf16[768,256]{1,0:T(8,128)(2,1)S(1)} %get-tuple-element.31), channel_id=1, source_target_pairs={{8,0},{16,8},{24,16},{32,24},{40,32},{48,40},{56,48},{64,56},{72,6... | collective-permute-start | bytes 1179656 | tf_op jit(solution)/shard_map/ppermute | solution.py:340
  37.1 9.5 %local_backward.1 = (bf16[768,1024]{1,0:T(8,128)(2,1)}, f32[768,256]{1,0:T(8,128)S(1)}) custom-call(s32[12]{0:T(128)S(1)} %pad_add_fusion.first_ref, bf16[768,1024]{1,0:T(8,128)(2,1)S(1)} %copy-done, bf16[768,1024]{1,0:T(8,128)(2,1)S(1)} %get-tuple-element.26.gs_ref, bf16[768,1024]{1,0:T(8,128)(2,1)} %get-tuple-element.15.out_ref, ...), custom_call_target="tpu_custom_call" | custom-call | flops 5368709120 | bytes 8388608 | tf_op jit(solution)/shard_map/local_backward/pallas_call | solution.py:291
  46.5 4.2 %collective-permute-done.1 = bf16[768,256]{1,0:T(8,128)(2,1)S(1)} collective-permute-done((bf16[768,256]{1,0:T(8,128)(2,1)S(1)}, bf16[768,256]{1,0:T(8,128)(2,1)S(1)}, u32[]{:S(2)}, u32[]{:S(2)}) %collective-permute-start.1) | collective-permute-done | bytes 393248 | tf_op jit(solution)/shard_map/ppermute | solution.py:340
  50.7 0.1 add_convert_fusion
  50.8 11.3 %all_to_all.10.x_ref = bf16[8,96,256]{2,1,0:T(8,128)(2,1)S(1)} all-to-all(bf16[8,96,256]{2,1,0:T(8,128)(2,1)S(1)} %bitcast.6), channel_id=1, replica_groups=mesh['ctx'=32,'dp'=8] {'dp'}, dimensions={0} | all-to-all | bytes 786432 | tf_op jit(solution)/shard_map/all_to_all | solution.py:367
  62.1 0.9 %unpack_heads.1 = (bf16[96,1024]{1,0:T(8,128)(2,1)}, bf16[96,1024]{1,0:T(8,128)(2,1)}) custom-call(bf16[8,96,256]{2,1,0:T(8,128)(2,1)S(1)} %all_to_all.10.x_ref), custom_call_target="tpu_custom_call" | custom-call | tf_op jit(solution)/shard_map/unpack_heads/pallas_call | solution.py:329
  (6 shorter events, 0.0 us)
Async XLA Ops:
  0.6 6.2 %copy-start.2 = (s32[64]{0:T(128)S(1)}, s32[64]{0:T(128)}, u32[]{:S(2)}) copy-start(s32[64]{0:T(128)} %param.9) | copy-start | bytes 772
  0.6 17.9 %copy-start = (bf16[768,1024]{1,0:T(8,128)(2,1)S(1)}, bf16[768,1024]{1,0:T(8,128)(2,1)}, u32[]{:S(2)}) copy-start(bf16[768,1024]{1,0:T(8,128)(2,1)} %q_ref.5) | copy-start | bytes 4718596
  2.5 13.2 %all-to-all-start = ((bf16[8,96,256]{2,1,0:T(8,128)(2,1)}), bf16[8,96,256]{2,1,0:T(8,128)(2,1)S(1)}, u32[]{:S(2)}, u32[]{:S(2)}) async-start(bf16[8,96,256]{2,1,0:T(8,128)(2,1)} %pack_heads.1), calls=%async_computation | async-start | bytes 786432 | tf_op jit(solution)/shard_map/all_to_all | solution.py:346
  15.8 11.2 %collective-permute-start = (bf16[768,256]{1,0:T(8,128)(2,1)S(1)}, bf16[768,256]{1,0:T(8,128)(2,1)S(1)}, u32[]{:S(2)}, u32[]{:S(2)}) collective-permute-start(bf16[768,256]{1,0:T(8,128)(2,1)S(1)} %bitcast.3), channel_id=1, source_target_pairs={{0,8},{8,16},{16,24},{24,32},{32,40},{40,48},{48,56},{56,64},{64,7... | collective-permute-start | bytes 1179656 | tf_op jit(solution)/shard_map/ppermute | solution.py:340
  18.6 8.4 %copy-start.1 = (bf16[768,1024]{1,0:T(8,128)(2,1)S(1)}, bf16[768,1024]{1,0:T(8,128)(2,1)}, u32[]{:S(2)}) copy-start(bf16[768,1024]{1,0:T(8,128)(2,1)} %g_ref.3) | copy-start | bytes 4718596
  35.1 15.6 %collective-permute-start.1 = (bf16[768,256]{1,0:T(8,128)(2,1)S(1)}, bf16[768,256]{1,0:T(8,128)(2,1)S(1)}, u32[]{:S(2)}, u32[]{:S(2)}) collective-permute-start(bf16[768,256]{1,0:T(8,128)(2,1)S(1)} %get-tuple-element.31), channel_id=1, source_target_pairs={{8,0},{16,8},{24,16},{32,24},{40,32},{48,40},{56,48},{64,56},{72,6... | collective-permute-start | bytes 1179656 | tf_op jit(solution)/shard_map/ppermute | solution.py:340
